TPU v7x, 32 devices: a whole 2x2x4 slice. The times are simulated.
32 devices in a mesh: blk: 8 (over z, x), pair: 4 (over y, core).
Axes of the slice: x: 2, y: 2, z: 4, core: 2. Of those that a mesh axis runs over, the one named last changes fastest.
Arguments:
- records: bfloat16 [8, 1024, 2048], P('blk', 'pair'), may hold values from -100 to 100
- offsets: int32 [2], replicated, may hold values from 1 to 7, as said below
- source_side: int32 [8, 2], P('blk'), may hold values from 0 to 1
Outputs:
- first_side: bfloat16 [8, 2, 32, 128, 128], P('blk', None, 'pair')
- second_side: bfloat16 [8, 2, 32, 128, 128], P('blk', None, 'pair')
Inputs may be any that keep to these rules, and one draw needn't show every extreme that they name: `offsets`: distinct and increasing; the last one is 7.
All inputs are finite; a program needn't handle non-finite values.
Results may differ from a plain program's by a relative error of at most 0.012.
Values may be sent and summed in bfloat16 or wider, within the bound.
No kernel may reach another device: no remote copies, remote signals or barrier semaphores. Data moves between devices by JAX's collectives and lax.ppermute only.
A program may use at most 128 MiB of HBM per device.

v0:
```python
import math
import jax
import jax.numpy as jnp
from jax import lax
from jax.sharding import PartitionSpec as P

BLOCK_CH = 128
BINS = 128
SAMPLES = 2048
FIRST_BIN = 4
LAGS = 32


def as_sent(value):
    return jax.tree.map(lambda a: a.astype(jnp.bfloat16) if a.dtype == jnp.float32 else a, value)


def shifted_2(value, axis, steps):
    count = lax.axis_size(axis)
    leading, last = (max(0, -steps), min(count, count - steps))
    return lax.ppermute(value, axis, [(source, source + steps) for source in range(leading, last)])


def fourier_table():
    sample_index = jnp.arange(SAMPLES, dtype=jnp.int32)
    bin_index = FIRST_BIN + jnp.arange(BINS, dtype=jnp.int32)
    phase_index = sample_index[:, None] * bin_index[None, :] % SAMPLES
    angles = 2.0 * math.pi / SAMPLES * phase_index.astype(jnp.float32)
    hann_taper = 0.5 - 0.5 * jnp.cos(2.0 * math.pi / SAMPLES * sample_index.astype(jnp.float32))
    return jnp.stack(
        (hann_taper[:, None] * jnp.cos(angles), -hann_taper[:, None] * jnp.sin(angles)), axis=-1
    )


def shift_ahead(distance):
    return lambda block: jax.tree.map(
        lambda part, own: part.astype(own.dtype), shifted_2(as_sent(block), "blk", -distance), block
    )


def local(records, offsets, source_side):
    seg_local = records.shape[0]
    local_blocks = records.shape[1] // BLOCK_CH
    table_full = fourier_table()
    table_high = lax.optimization_barrier(table_full.astype(jnp.bfloat16))
    table_low = (table_full - table_high.astype(jnp.float32)).astype(jnp.bfloat16)
    traces = records.reshape(seg_local, local_blocks, BLOCK_CH, SAMPLES)
    spectrum = jnp.einsum("sbcn,nfr->bfsrc", traces, table_high, preferred_element_type=jnp.float32)
    spectrum = spectrum + jnp.einsum(
        "sbcn,nfr->bfsrc", traces, table_low, preferred_element_type=jnp.float32
    )
    band_power = jnp.sum(spectrum * spectrum, axis=3)
    band_level = jnp.mean(band_power, axis=-1)
    whiten_scale = 1.0 / jnp.sqrt(band_level + 1e-05)
    whitened = (spectrum * whiten_scale[:, :, :, None, None]).astype(jnp.bfloat16)
    regrouped = lax.all_to_all(
        lax.all_to_all(whitened, "pair", split_axis=1, concat_axis=0, tiled=True),
        "blk",
        split_axis=0,
        concat_axis=2,
        tiled=True,
    )
    own_block = regrouped[0]
    bin_local = own_block.shape[0]
    seg_total = own_block.shape[1]
    offset_total = offsets.shape[0]
    group_size = lax.axis_size("blk")
    window_size = min(16, group_size)
    bit_total = window_size.bit_length() - 1
    ahead_list = [shift_ahead(distance) for distance in range(1, window_size)]
    partners = jnp.stack(
        [lax.switch(offsets[slot] - 1, ahead_list, own_block) for slot in range(offset_total)]
    )
    reverse_side = (source_side[0] == 1)[:, None, None, None, None]
    own_many = jnp.broadcast_to(own_block[None], partners.shape)
    source = jnp.where(reverse_side, partners, own_many)
    receiver = jnp.where(reverse_side, own_many, partners)
    left_side = source.reshape(offset_total, bin_local, 2 * seg_total, BLOCK_CH)
    rotated = jnp.stack((receiver[:, :, :, 1], -receiver[:, :, :, 0]), axis=3)
    right_side = jnp.stack((receiver, rotated), axis=4).reshape(
        offset_total, bin_local, 2 * seg_total, 2, BLOCK_CH
    )
    cross = jnp.einsum(
        "kfsc,kfsrd->kfrcd", left_side, right_side, preferred_element_type=jnp.float32
    )
    cross_rows = cross.reshape(offset_total, 2 * bin_local, BLOCK_CH * BLOCK_CH)
    pair_index = lax.axis_index("pair")
    lag_index = jnp.arange(LAGS, dtype=jnp.int32) - LAGS // 2
    bin_index = FIRST_BIN + pair_index * bin_local + jnp.arange(bin_local, dtype=jnp.int32)
    phase_index = lag_index[:, None] * bin_index[None, :] % SAMPLES
    angles = 2.0 * math.pi / SAMPLES * phase_index.astype(jnp.float32)
    normalizer = 1.0 / math.sqrt(seg_total * BINS)
    lag_table = (jnp.stack((jnp.cos(angles), -jnp.sin(angles)), axis=-1) * normalizer).reshape(
        LAGS, 2 * bin_local
    )
    summed = lax.psum_scatter(
        jnp.einsum(
            "lq,kqx->lkx",
            lag_table,
            cross_rows,
            precision=lax.Precision.HIGHEST,
            preferred_element_type=jnp.float32,
        ).astype(jnp.bfloat16),
        "pair",
        scatter_dimension=0,
        tiled=True,
    ).astype(jnp.float32)
    lag_local = summed.shape[0]
    first_local = (
        summed.astype(jnp.bfloat16)
        .transpose(1, 0, 2)
        .reshape(offset_total, lag_local, BLOCK_CH, BLOCK_CH)
    )
    returned = first_local
    for bit_number in range(bit_total):
        shifted = shifted_2(returned, "blk", 1 << bit_number)
        selected = (jnp.right_shift(offsets, bit_number) % 2 == 1)[:, None, None, None]
        returned = jnp.where(selected, shifted, returned)
    return (first_local[None], returned[None])


def solution(mesh):
    placed = (P("blk", "pair", None), P(), P("blk", None))
    return jax.shard_map(
        local,
        mesh=mesh,
        in_specs=placed,
        out_specs=(P("blk", None, "pair", None, None), P("blk", None, "pair", None, None)),
        check_vma=False,
    )
```

profile of v0, /device:TPU:25, one launch (start us, length us, event | category | flops | bytes accessed | tf_op | source)
XLA Modules:
  0.0 181.7 jit_solution(7638834543979147514)
XLA Ops:
  7.2 4.2 %cosine_multiply_fusion = (f32[2048,128,1]{1,0,2:T(8,128)S(1)}, f32[2048,128,1]{1,0,2:T(8,128)S(1)}) fusion(s32[128]{0:T(128)S(1)} %iota_add_fusion, f32[2048]{0:T(1024)S(1)} %get-tuple-element.57, f32[2048]{0:T(1024)S(1)} %get-tuple-element.58), kind=kLoop, calls=%fused_computation.18 | loop fusion | flops 4194304 | bytes 2114048 | tf_op jit(solution)/shard_map/mul | solution.py:31
  13.4 4.0 %all-to-all-start = ((bf16[2,128,1,2,128]{4,0,3,2,1:T(2,128)(2,1)}), bf16[2,128,1,2,128]{4,0,3,2,1:T(2,128)(2,1)S(1)}, u32[]{:S(2)}, u32[]{:S(2)}) async-start(bf16[2,128,1,2,128]{4,0,3,2,1:T(2,128)(2,1)} %copy.65), calls=%async_computation | async-start | bytes 262144 | tf_op jit(solution)/shard_map/all_to_all | solution.py:57
  17.6 3.4 %all-to-all-done = bf16[2,128,1,2,128]{4,0,3,2,1:T(2,128)(2,1)S(1)} async-done(((bf16[2,128,1,2,128]{4,0,3,2,1:T(2,128)(2,1)}), bf16[2,128,1,2,128]{4,0,3,2,1:T(2,128)(2,1)S(1)}, u32[]{:S(2)}, u32[]{:S(2)}) %all-to-all-start) | async-done | bytes 131104 | tf_op jit(solution)/shard_map/all_to_all | solution.py:57
  21.6 5.5 %all-to-all-start.1 = ((bf16[8,32,1,2,128]{4,1,3,2,0:T(8,128)(2,1)}), bf16[8,32,1,2,128]{4,1,3,2,0:T(8,128)(2,1)S(1)}, u32[]{:S(2)}, u32[]{:S(2)}) async-start(bf16[8,32,1,2,128]{4,1,3,2,0:T(8,128)(2,1)} %bitcast.15), calls=%async_computation.1 | async-start | bytes 262144 | tf_op jit(solution)/shard_map/all_to_all | solution.py:56
  29.0 1.6 all-to-all-done.1
  30.7 4.9 %conditional.2 = (bf16[32,8,2,128]{3,2,1,0:T(2,128)(2,1)}) conditional(s32[]{:T(128)} %bitcast.19, bf16[32,8,2,128]{3,2,1,0:T(2,128)(2,1)S(1)} %copy.69, bf16[32,8,2,128]{3,2,1,0:T(2,128)(2,1)S(1)} %copy.69, bf16[32,8,2,128]{3,2,1,0:T(2,128)(2,1)S(1)} %copy.69, bf16[32,8,2,128]{3,2,1,0:T(2,128)(2,1)S(1)} %copy.69, ...), branch_computations={%region_1.2_spmd, %region_2.3_spmd, %region_3.4_spmd, %region_4.5_... | conditional | bytes 524336 | solution.py:72
  30.7 3.6 %collective-permute-start.1 = (bf16[32,8,2,128]{3,2,1,0:T(2,128)(2,1)S(1)}, bf16[32,8,2,128]{3,2,1,0:T(2,128)(2,1)}, u32[]{:S(2)}, u32[]{:S(2)}) collective-permute-start(bf16[32,8,2,128]{3,2,1,0:T(2,128)(2,1)S(1)} %param.1), channel_id=1, source_target_pairs={{8,0},{12,4},{16,8},{20,12},{24,16},{28,20},{9,1},{13,5},{17,9},{2... | collective-permute-start | bytes 393224 | tf_op jit(solution)/shard_map/cond/branch_1_fun/ppermute | solution.py:21
  34.3 1.3 collective-permute-done.1
  35.6 1.3 conditional.3
  35.6 1.3 collective-permute-start.13
  37.0 1.4 broadcast_select_fusion
  40.6 5.5 %convolution_bitcast_fusion = f32[2,32,2,128,128]{3,4,2,1,0:T(8,128)} fusion(bf16[2,32,16,1,128]{4,2,3,1,0:T(8,128)(2,1)S(1)} %bitcast.79, bf16[2,32,16,1,128]{4,2,3,1,0:T(8,128)(2,1)S(1)} %maximum_select_fusion, bf16[1,32,16,128]{3,2,1,0:T(8,128)(2,1)} %bitcast.30, bf16[1,32,16,128]{3,2,1,0:T(8,128)(2,1)} %bitcast.29, ...), kind=kOutput, calls=%fused_computation.2 | convolution fusion | flops 67633152 | bytes 9306114 | tf_op jit(solution)/shard_map/kfsc,kfsrd->kfrcd/dot_general | solution.py:83
  46.1 8.9 %copy.85 = f32[2,32,2,128,128]{4,3,2,1,0:T(8,128)} copy(f32[2,32,2,128,128]{3,4,2,1,0:T(8,128)} %convolution_bitcast_fusion) | data formatting | bytes 16777216 | tf_op jit(solution)/shard_map/kfsc,kfsrd->kfrcd/transpose | solution.py:83
  55.0 9.4 %reshape.414 = f32[2,64,16384]{2,1,0:T(8,128)} reshape(f32[2,32,2,128,128]{4,3,2,1,0:T(8,128)} %copy.85) | data formatting | bytes 16777216 | tf_op jit(solution)/shard_map/reshape | solution.py:86
  64.4 6.4 %fusion = bf16[2,4,8,16384]{3,2,1,0:T(8,128)(2,1)S(1)} fusion(f32[32,64,1]{0,1,2:T(8,128)S(1)} %bitcast.81, f32[2,64,16384]{2,1,0:T(8,128)} %reshape.414), kind=kOutput, calls=%fused_computation.1 | convolution fusion | flops 806354944 | bytes 10493952 | tf_op jit(solution)/shard_map/lq,kqx->lkx/dot_general | solution.py:97
  70.9 1.5 copy.97
  72.4 42.0 %reduce-scatter.4.cloned.1.call-done = bf16[8,32768]{1,0:T(8,128)(2,1)} async-done(((bf16[32,32768]{1,0:T(8,128)(2,1)}), bf16[8,32768]{1,0:T(8,128)(2,1)}) %reduce-scatter.4.cloned.1.call-update) | async-done | bytes 524304
  114.4 1.2 copy.87
  115.6 3.1 %collective-permute-start.14 = (bf16[2,8,128,128]{3,2,1,0:T(8,128)(2,1)S(1)}, bf16[2,8,128,128]{3,2,1,0:T(8,128)(2,1)S(1)}, u32[]{:S(2)}, u32[]{:S(2)}) collective-permute-start(bf16[2,8,128,128]{3,2,1,0:T(8,128)(2,1)S(1)} %copy.87), channel_id=1, source_target_pairs={{0,4},{4,8},{8,12},{12,16},{16,20},{20,24},{24,28},{1,5},{5,9},{9,... | collective-permute-start | bytes 1572872 | tf_op jit(solution)/shard_map/ppermute | solution.py:21
  118.8 12.3 %collective-permute-done.14 = bf16[2,8,128,128]{3,2,1,0:T(8,128)(2,1)S(1)} collective-permute-done((bf16[2,8,128,128]{3,2,1,0:T(8,128)(2,1)S(1)}, bf16[2,8,128,128]{3,2,1,0:T(8,128)(2,1)S(1)}, u32[]{:S(2)}, u32[]{:S(2)}) %collective-permute-start.14) | collective-permute-done | bytes 524320 | tf_op jit(solution)/shard_map/ppermute | solution.py:21
  132.2 1.3 collective-permute-start.15
  133.5 12.4 %collective-permute-done.15 = bf16[2,8,128,128]{3,2,1,0:T(8,128)(2,1)S(1)} collective-permute-done((bf16[2,8,128,128]{3,2,1,0:T(8,128)(2,1)S(1)}, bf16[2,8,128,128]{3,2,1,0:T(8,128)(2,1)S(1)}, u32[]{:S(2)}, u32[]{:S(2)}) %collective-permute-start.15) | collective-permute-done | bytes 524320 | tf_op jit(solution)/shard_map/ppermute | solution.py:21
  146.0 1.3 collective-permute-start.16
  148.2 25.7 %collective-permute-done.16 = bf16[2,8,128,128]{3,2,1,0:T(8,128)(2,1)S(1)} collective-permute-done((bf16[2,8,128,128]{3,2,1,0:T(8,128)(2,1)S(1)}, bf16[2,8,128,128]{3,2,1,0:T(8,128)(2,1)S(1)}, u32[]{:S(2)}, u32[]{:S(2)}) %collective-permute-start.16) | collective-permute-done | bytes 524320 | tf_op jit(solution)/shard_map/ppermute | solution.py:21
  (37 shorter events, 8.9 us)
Async XLA Ops:
  7.2 4.4 %copy-start = (bf16[1,256,2048]{2,1,0:T(8,128)(2,1)S(1)}, bf16[1,256,2048]{2,1,0:T(8,128)(2,1)}, u32[]{:S(2)}) copy-start(bf16[1,256,2048]{2,1,0:T(8,128)(2,1)} %param.17) | copy-start | bytes 3145732
  11.6 15.5 %copy-start.2 = (s32[2]{0:T(128)S(1)}, s32[2]{0:T(128)}, u32[]{:S(2)}) copy-start(s32[2]{0:T(128)} %param.18) | copy-start | bytes 28
  11.6 17.4 %copy-start.3 = (s32[1,2]{1,0:T(1,128)S(1)}, s32[1,2]{1,0:T(1,128)}, u32[]{:S(2)}) copy-start(s32[1,2]{1,0:T(1,128)} %param.19) | copy-start | bytes 28
  13.4 7.5 %all-to-all-start = ((bf16[2,128,1,2,128]{4,0,3,2,1:T(2,128)(2,1)}), bf16[2,128,1,2,128]{4,0,3,2,1:T(2,128)(2,1)S(1)}, u32[]{:S(2)}, u32[]{:S(2)}) async-start(bf16[2,128,1,2,128]{4,0,3,2,1:T(2,128)(2,1)} %copy.65), calls=%async_computation | async-start | bytes 262144 | tf_op jit(solution)/shard_map/all_to_all | solution.py:57
  21.6 8.9 %all-to-all-start.1 = ((bf16[8,32,1,2,128]{4,1,3,2,0:T(8,128)(2,1)}), bf16[8,32,1,2,128]{4,1,3,2,0:T(8,128)(2,1)S(1)}, u32[]{:S(2)}, u32[]{:S(2)}) async-start(bf16[8,32,1,2,128]{4,1,3,2,0:T(8,128)(2,1)} %bitcast.15), calls=%async_computation.1 | async-start | bytes 262144 | tf_op jit(solution)/shard_map/all_to_all | solution.py:56
  27.1 87.3 %reduce-scatter.4.cloned.1.call-start = ((), (), s32[]{:S(2)}) async-start(), calls=%async_computation.3 | async-start | bytes 2621440
  30.7 4.9 %collective-permute-start.1 = (bf16[32,8,2,128]{3,2,1,0:T(2,128)(2,1)S(1)}, bf16[32,8,2,128]{3,2,1,0:T(2,128)(2,1)}, u32[]{:S(2)}, u32[]{:S(2)}) collective-permute-start(bf16[32,8,2,128]{3,2,1,0:T(2,128)(2,1)S(1)} %param.1), channel_id=1, source_target_pairs={{8,0},{12,4},{16,8},{20,12},{24,16},{28,20},{9,1},{13,5},{17,9},{2... | collective-permute-start | bytes 393224 | tf_op jit(solution)/shard_map/cond/branch_1_fun/ppermute | solution.py:21
  35.6 1.3 collective-permute-start.13
  114.4 32.9 %copy-start.1 = (bf16[8,32768]{1,0:T(8,128)(2,1)S(1)}, bf16[8,32768]{1,0:T(8,128)(2,1)}, u32[]{:S(2)}) copy-start(bf16[8,32768]{1,0:T(8,128)(2,1)} %reduce-scatter.4.cloned.1.call-done) | copy-start | bytes 1572868
  115.6 15.4 %collective-permute-start.14 = (bf16[2,8,128,128]{3,2,1,0:T(8,128)(2,1)S(1)}, bf16[2,8,128,128]{3,2,1,0:T(8,128)(2,1)S(1)}, u32[]{:S(2)}, u32[]{:S(2)}) collective-permute-start(bf16[2,8,128,128]{3,2,1,0:T(8,128)(2,1)S(1)} %copy.87), channel_id=1, source_target_pairs={{0,4},{4,8},{8,12},{12,16},{16,20},{20,24},{24,28},{1,5},{5,9},{9,... | collective-permute-start | bytes 1572872 | tf_op jit(solution)/shard_map/ppermute | solution.py:21
  132.2 13.7 %collective-permute-start.15 = (bf16[2,8,128,128]{3,2,1,0:T(8,128)(2,1)S(1)}, bf16[2,8,128,128]{3,2,1,0:T(8,128)(2,1)S(1)}, u32[]{:S(2)}, u32[]{:S(2)}) collective-permute-start(bf16[2,8,128,128]{3,2,1,0:T(8,128)(2,1)S(1)} %broadcast_select_fusion.1), channel_id=1, source_target_pairs={{0,8},{4,12},{8,16},{12,20},{16,24},{20,28},{1,9},{5,13},{9,17},{1... | collective-permute-start | bytes 1572872 | tf_op jit(solution)/shard_map/ppermute | solution.py:21
  146.0 27.9 %collective-permute-start.16 = (bf16[2,8,128,128]{3,2,1,0:T(8,128)(2,1)S(1)}, bf16[2,8,128,128]{3,2,1,0:T(8,128)(2,1)S(1)}, u32[]{:S(2)}, u32[]{:S(2)}) collective-permute-start(bf16[2,8,128,128]{3,2,1,0:T(8,128)(2,1)S(1)} %broadcast_select_fusion.2), channel_id=1, source_target_pairs={{0,16},{4,20},{8,24},{12,28},{1,17},{5,21},{9,25},{13,29},{2,18},{... | collective-permute-start | bytes 1572872 | tf_op jit(solution)/shard_map/ppermute | solution.py:21
Sparse Core Ops, SparseCore 0:
  72.5 41.8 reduce-scatter.3
where the time goes:
time: 183 us; the launch traced here: 182 us
  waiting for transfers between devices  98.6 us (54%)
  local copies, waits for them, and re-layouts  24.2 us (13%)
  starting transfers between devices  20 us (11%)
  between operations  15.4 us (8%)
  matrix products  12.9 us (7%)
  other arithmetic  10.4 us (6%)
    ppermute x5, waiting for transfers between devices, shifted_2(): lax.ppermute(value, axis, [(source, source + steps) for source in range(l...  51.6 us
    unnamed x2, waiting for transfers between devices  42 us
    ppermute x5, starting transfers between devices, shifted_2(): lax.ppermute(value, axis, [(source, source + steps) for source in range(l...  10.6 us
    reshape x1, local copies, waits for them, and re-layouts, local(): cross_rows = cross.reshape(offset_total, 2 * bin_local, BLOCK_CH * BLOCK_CH)  9.44 us
    transpose x1, local copies, waits for them, and re-layouts, local(): jnp.einsum('kfsc,kfsrd->kfrcd', left_side, right_side, preferred_element_...  8.89 us
    dot_general x1, matrix products, local(): jnp.einsum('lq,kqx->lkx', lag_table, cross_rows, precision=lax.Precision....  6.43 us
    dot_general x1, matrix products, local(): jnp.einsum('kfsc,kfsrd->kfrcd', left_side, right_side, preferred_element_...  5.54 us
    all_to_all x1, starting transfers between devices, local(): lax.all_to_all(lax.all_to_all(whitened, 'pair', split_axis=1, concat_axis...  5.46 us
  transfers between devices with their start and end apart: 8, of which 7 were waited for; matrix products, arithmetic and copies ran while one was open for 1% of the time, Pallas kernels for 0%

commit v1 on v0

--- a/solution.py
+++ b/solution.py
@@ -9,6 +9,18 @@
 SAMPLES = 2048
 FIRST_BIN = 4
 LAGS = 32
+
+
+def cut_along(x, dim, size):
+    dims = x.shape
+    parts = x.reshape(*dims[:dim], size, dims[dim] // size, *dims[dim + 1 :])
+    return jnp.moveaxis(parts, dim, 0)
+
+
+def laid_out(pieces, dim):
+    pieces = jnp.moveaxis(pieces, 0, dim)
+    dims = pieces.shape
+    return pieces.reshape(*dims[:dim], dims[dim] * dims[dim + 1], *dims[dim + 2 :])
 
 
 def as_sent(value):
@@ -53,13 +65,15 @@
     band_level = jnp.mean(band_power, axis=-1)
     whiten_scale = 1.0 / jnp.sqrt(band_level + 1e-05)
     whitened = (spectrum * whiten_scale[:, :, :, None, None]).astype(jnp.bfloat16)
-    regrouped = lax.all_to_all(
-        lax.all_to_all(whitened, "pair", split_axis=1, concat_axis=0, tiled=True),
-        "blk",
-        split_axis=0,
-        concat_axis=2,
-        tiled=True,
-    )
+    x = lax.all_to_all(whitened, "pair", split_axis=1, concat_axis=0, tiled=True)
+    size, index = (lax.axis_size("blk"), lax.axis_index("blk"))
+    blocks = cut_along(x, 0, size)
+    done = [blocks[index]]
+    for step in range(1, size):
+        sent = blocks[index ^ step]
+        done.append(lax.ppermute(sent, "blk", [(i, i ^ step) for i in range(size)]))
+    blocks = jnp.stack(done)[index ^ jnp.arange(size)]
+    regrouped = laid_out(blocks, 2)
     own_block = regrouped[0]
     bin_local = own_block.shape[0]
     seg_total = own_block.shape[1]

time: 183 us -> 187 us (1.022)
  waiting for transfers between devices: 98.6 us -> 101 us
  starting transfers between devices: 20 us -> 22.2 us
    ppermute x0 -> x7, starting transfers between devices: none -> 9.23 us  [local(): done.append(lax.ppermute(sent, 'blk', [(i, i ^ step) for i in range(size)]))]
    all_to_all x1 -> x0, starting transfers between devices: 5.46 us -> none  [local(): lax.all_to_all(lax.all_to_all(whitened, 'pair', split_axis=1, concat_axis...]
    unnamed x2, waiting for transfers between devices: 42 us -> 45.5 us
    ppermute x0 -> x7, waiting for transfers between devices: none -> 2.17 us  [local(): done.append(lax.ppermute(sent, 'blk', [(i, i ^ step) for i in range(size)]))]
    all_to_all x1, waiting for transfers between devices: 3.39 us -> 1.43 us  [local(): lax.all_to_all(whitened, 'pair', split_axis=1, concat_axis=0, tiled=True)]
  transfers between devices with their start and end apart: 8 -> 14, of which waited for: 7 -> 8; matrix products, arithmetic and copies ran while one was open for 1% -> 1% of each run, Pallas kernels for 0% -> 0%
where the time goes in v1:
time: 187 us; the launch traced here: 186 us
  waiting for transfers between devices  101 us (54%)
  local copies, waits for them, and re-layouts  24.2 us (13%)
  starting transfers between devices  22.2 us (12%)
  between operations  15.5 us (8%)
  matrix products  12.9 us (7%)
  other arithmetic  10.4 us (6%)
    ppermute x5, waiting for transfers between devices, shifted_2(): lax.ppermute(value, axis, [(source, source + steps) for source in range(l...  51.6 us
    unnamed x2, waiting for transfers between devices  45.5 us
    reshape x1, local copies, waits for them, and re-layouts, local(): cross_rows = cross.reshape(offset_total, 2 * bin_local, BLOCK_CH * BLOCK_CH)  9.45 us
    ppermute x7, starting transfers between devices, local(): done.append(lax.ppermute(sent, 'blk', [(i, i ^ step) for i in range(size)]))  9.23 us
    ppermute x5, starting transfers between devices, shifted_2(): lax.ppermute(value, axis, [(source, source + steps) for source in range(l...  8.96 us
    transpose x1, local copies, waits for them, and re-layouts, local(): jnp.einsum('kfsc,kfsrd->kfrcd', left_side, right_side, preferred_element_...  8.87 us
    dot_general x1, matrix products, local(): jnp.einsum('lq,kqx->lkx', lag_table, cross_rows, precision=lax.Precision....  6.43 us
    dot_general x1, matrix products, local(): jnp.einsum('kfsc,kfsrd->kfrcd', left_side, right_side, preferred_element_...  5.55 us
  transfers between devices with their start and end apart: 14, of which 8 were waited for; matrix products, arithmetic and copies ran while one was open for 1% of the time, Pallas kernels for 0%

profile of v1, /device:TPU:25, one launch (start us, length us, event | category | flops | bytes accessed | tf_op | source)
XLA Modules:
  0.0 186.0 jit_solution(10682119108997970406)
XLA Ops:
  7.2 4.2 %cosine_multiply_fusion = (f32[2048,128,1]{1,0,2:T(8,128)S(1)}, f32[2048,128,1]{1,0,2:T(8,128)S(1)}) fusion(s32[128]{0:T(128)S(1)} %iota_add_fusion, f32[2048]{0:T(1024)S(1)} %get-tuple-element.62, f32[2048]{0:T(1024)S(1)} %get-tuple-element.63), kind=kLoop, calls=%fused_computation.19 | loop fusion | flops 4194304 | bytes 2114048 | tf_op jit(solution)/shard_map/mul | solution.py:43
  13.4 4.0 %all-to-all-start = ((bf16[2,128,1,2,128]{4,0,3,2,1:T(2,128)(2,1)}), bf16[2,128,1,2,128]{4,0,3,2,1:T(2,128)(2,1)S(1)}, u32[]{:S(2)}, u32[]{:S(2)}) async-start(bf16[2,128,1,2,128]{4,0,3,2,1:T(2,128)(2,1)} %copy.60), calls=%async_computation | async-start | bytes 262144 | tf_op jit(solution)/shard_map/all_to_all | solution.py:68
  19.5 1.4 all-to-all-done
  21.0 1.3 collective-permute-start.14
  23.8 3.2 %collective-permute-start.18 = (bf16[1,32,1,2,128]{4,1,3,2,0:T(8,128)(2,1)S(1)}, bf16[1,32,1,2,128]{4,1,3,2,0:T(8,128)(2,1)S(1)}, u32[]{:S(2)}, u32[]{:S(2)}) collective-permute-start(bf16[1,32,1,2,128]{4,1,3,2,0:T(8,128)(2,1)S(1)} %get-tuple-element.44), channel_id=1, source_target_pairs={{0,20},{4,16},{8,28},{12,24},{16,4},{20,0},{24,12},{28,8},{1,21},{... | collective-permute-start | bytes 49160 | tf_op jit(solution)/shard_map/ppermute | solution.py:74
  27.1 3.2 %collective-permute-start.20 = (bf16[1,32,1,2,128]{4,1,3,2,0:T(8,128)(2,1)S(1)}, bf16[1,32,1,2,128]{4,1,3,2,0:T(8,128)(2,1)S(1)}, u32[]{:S(2)}, u32[]{:S(2)}) collective-permute-start(bf16[1,32,1,2,128]{4,1,3,2,0:T(8,128)(2,1)S(1)} %get-tuple-element.42), channel_id=1, source_target_pairs={{0,28},{4,24},{8,20},{12,16},{16,12},{20,8},{24,4},{28,0},{1,29},{... | collective-permute-start | bytes 49160 | tf_op jit(solution)/shard_map/ppermute | solution.py:74
  33.2 3.3 %conditional.2 = (bf16[32,8,2,128]{3,2,1,0:T(2,128)(2,1)}) conditional(s32[]{:T(128)} %bitcast.36, bf16[32,8,2,128]{3,2,1,0:T(2,128)(2,1)S(1)} %copy.65, bf16[32,8,2,128]{3,2,1,0:T(2,128)(2,1)S(1)} %copy.65, bf16[32,8,2,128]{3,2,1,0:T(2,128)(2,1)S(1)} %copy.65, bf16[32,8,2,128]{3,2,1,0:T(2,128)(2,1)S(1)} %copy.65, ...), branch_computations={%region_1.2_spmd, %region_2.3_spmd, %region_3.4_spmd, %region_4.5_... | conditional | bytes 524336 | solution.py:86
  33.2 2.0 %collective-permute-start.1 = (bf16[32,8,2,128]{3,2,1,0:T(2,128)(2,1)S(1)}, bf16[32,8,2,128]{3,2,1,0:T(2,128)(2,1)}, u32[]{:S(2)}, u32[]{:S(2)}) collective-permute-start(bf16[32,8,2,128]{3,2,1,0:T(2,128)(2,1)S(1)} %param.1), channel_id=1, source_target_pairs={{8,0},{12,4},{16,8},{20,12},{24,16},{28,20},{9,1},{13,5},{17,9},{2... | collective-permute-start | bytes 393224 | tf_op jit(solution)/shard_map/cond/branch_1_fun/ppermute | solution.py:33
  35.2 1.3 collective-permute-done.1
  36.5 1.3 conditional.3
  36.5 1.3 collective-permute-start.13
  37.8 1.4 broadcast_select_fusion
  41.4 5.5 %convolution_bitcast_fusion = f32[2,32,2,128,128]{3,4,2,1,0:T(8,128)} fusion(bf16[2,32,16,1,128]{4,2,3,1,0:T(8,128)(2,1)S(1)} %bitcast.112, bf16[2,32,16,1,128]{4,2,3,1,0:T(8,128)(2,1)S(1)} %maximum_select_fusion, bf16[1,32,16,128]{3,2,1,0:T(8,128)(2,1)} %bitcast.47, bf16[1,32,16,128]{3,2,1,0:T(8,128)(2,1)} %bitcast.46, ...), kind=kOutput, calls=%fused_computation.3 | convolution fusion | flops 67633152 | bytes 9306114 | tf_op jit(solution)/shard_map/kfsc,kfsrd->kfrcd/dot_general | solution.py:97
  47.0 8.9 %copy.81 = f32[2,32,2,128,128]{4,3,2,1,0:T(8,128)} copy(f32[2,32,2,128,128]{3,4,2,1,0:T(8,128)} %convolution_bitcast_fusion) | data formatting | bytes 16777216 | tf_op jit(solution)/shard_map/kfsc,kfsrd->kfrcd/transpose | solution.py:97
  55.9 9.4 %reshape.434 = f32[2,64,16384]{2,1,0:T(8,128)} reshape(f32[2,32,2,128,128]{4,3,2,1,0:T(8,128)} %copy.81) | data formatting | bytes 16777216 | tf_op jit(solution)/shard_map/reshape | solution.py:100
  65.3 6.4 %fusion = bf16[2,4,8,16384]{3,2,1,0:T(8,128)(2,1)S(1)} fusion(f32[32,64,1]{0,1,2:T(8,128)S(1)} %bitcast.117, f32[2,64,16384]{2,1,0:T(8,128)} %reshape.434), kind=kOutput, calls=%fused_computation.2 | convolution fusion | flops 806354944 | bytes 10493952 | tf_op jit(solution)/shard_map/lq,kqx->lkx/dot_general | solution.py:111
  71.8 1.5 copy.93
  73.3 45.5 %reduce-scatter.4.cloned.1.call-done = bf16[8,32768]{1,0:T(8,128)(2,1)} async-done(((bf16[32,32768]{1,0:T(8,128)(2,1)}), bf16[8,32768]{1,0:T(8,128)(2,1)}) %reduce-scatter.4.cloned.1.call-update) | async-done | bytes 524304
  120.0 3.1 %collective-permute-start.21 = (bf16[2,8,128,128]{3,2,1,0:T(8,128)(2,1)S(1)}, bf16[2,8,128,128]{3,2,1,0:T(8,128)(2,1)S(1)}, u32[]{:S(2)}, u32[]{:S(2)}) collective-permute-start(bf16[2,8,128,128]{3,2,1,0:T(8,128)(2,1)S(1)} %copy.83), channel_id=1, source_target_pairs={{0,4},{4,8},{8,12},{12,16},{16,20},{20,24},{24,28},{1,5},{5,9},{9,... | collective-permute-start | bytes 1572872 | tf_op jit(solution)/shard_map/ppermute | solution.py:33
  123.2 12.3 %collective-permute-done.21 = bf16[2,8,128,128]{3,2,1,0:T(8,128)(2,1)S(1)} collective-permute-done((bf16[2,8,128,128]{3,2,1,0:T(8,128)(2,1)S(1)}, bf16[2,8,128,128]{3,2,1,0:T(8,128)(2,1)S(1)}, u32[]{:S(2)}, u32[]{:S(2)}) %collective-permute-start.21) | collective-permute-done | bytes 524320 | tf_op jit(solution)/shard_map/ppermute | solution.py:33
  136.6 1.3 collective-permute-start.22
  137.9 12.4 %collective-permute-done.22 = bf16[2,8,128,128]{3,2,1,0:T(8,128)(2,1)S(1)} collective-permute-done((bf16[2,8,128,128]{3,2,1,0:T(8,128)(2,1)S(1)}, bf16[2,8,128,128]{3,2,1,0:T(8,128)(2,1)S(1)}, u32[]{:S(2)}, u32[]{:S(2)}) %collective-permute-start.22) | collective-permute-done | bytes 524320 | tf_op jit(solution)/shard_map/ppermute | solution.py:33
  150.4 1.3 collective-permute-start.23
  152.6 25.7 %collective-permute-done.23 = bf16[2,8,128,128]{3,2,1,0:T(8,128)(2,1)S(1)} collective-permute-done((bf16[2,8,128,128]{3,2,1,0:T(8,128)(2,1)S(1)}, bf16[2,8,128,128]{3,2,1,0:T(8,128)(2,1)S(1)}, u32[]{:S(2)}, u32[]{:S(2)}) %collective-permute-start.23) | collective-permute-done | bytes 524320 | tf_op jit(solution)/shard_map/ppermute | solution.py:33
  (61 shorter events, 13.8 us)
Async XLA Ops:
  7.2 4.4 %copy-start = (bf16[1,256,2048]{2,1,0:T(8,128)(2,1)S(1)}, bf16[1,256,2048]{2,1,0:T(8,128)(2,1)}, u32[]{:S(2)}) copy-start(bf16[1,256,2048]{2,1,0:T(8,128)(2,1)} %param.17) | copy-start | bytes 3145732
  11.6 5.8 %copy-start.2 = (s32[2]{0:T(128)S(1)}, s32[2]{0:T(128)}, u32[]{:S(2)}) copy-start(s32[2]{0:T(128)} %param.18) | copy-start | bytes 28
  11.6 7.6 %copy-start.3 = (s32[1,2]{1,0:T(1,128)S(1)}, s32[1,2]{1,0:T(1,128)}, u32[]{:S(2)}) copy-start(s32[1,2]{1,0:T(1,128)} %param.19) | copy-start | bytes 28
  13.4 7.5 %all-to-all-start = ((bf16[2,128,1,2,128]{4,0,3,2,1:T(2,128)(2,1)}), bf16[2,128,1,2,128]{4,0,3,2,1:T(2,128)(2,1)S(1)}, u32[]{:S(2)}, u32[]{:S(2)}) async-start(bf16[2,128,1,2,128]{4,0,3,2,1:T(2,128)(2,1)} %copy.60), calls=%async_computation | async-start | bytes 262144 | tf_op jit(solution)/shard_map/all_to_all | solution.py:68
  17.4 101.4 %reduce-scatter.4.cloned.1.call-start = ((), (), s32[]{:S(2)}) async-start(), calls=%async_computation.2 | async-start | bytes 2621440
  21.0 6.0 %collective-permute-start.14 = (bf16[1,32,1,2,128]{4,1,3,2,0:T(8,128)(2,1)S(1)}, bf16[1,32,1,2,128]{4,1,3,2,0:T(8,128)(2,1)S(1)}, u32[]{:S(2)}, u32[]{:S(2)}) collective-permute-start(bf16[1,32,1,2,128]{4,1,3,2,0:T(8,128)(2,1)S(1)} %get-tuple-element.48), channel_id=1, source_target_pairs={{0,4},{4,0},{8,12},{12,8},{16,20},{20,16},{24,28},{28,24},{1,5},{5... | collective-permute-start | bytes 49160 | tf_op jit(solution)/shard_map/ppermute | solution.py:74
  22.3 4.8 %collective-permute-start.15 = (bf16[1,32,1,2,128]{4,1,3,2,0:T(8,128)(2,1)S(1)}, bf16[1,32,1,2,128]{4,1,3,2,0:T(8,128)(2,1)S(1)}, u32[]{:S(2)}, u32[]{:S(2)}) collective-permute-start(bf16[1,32,1,2,128]{4,1,3,2,0:T(8,128)(2,1)S(1)} %get-tuple-element.47), channel_id=1, source_target_pairs={{0,8},{4,12},{8,0},{12,4},{16,24},{20,28},{24,16},{28,20},{1,9},{5... | collective-permute-start | bytes 49160 | tf_op jit(solution)/shard_map/ppermute | solution.py:74
  22.5 7.8 %collective-permute-start.16 = (bf16[1,32,1,2,128]{4,1,3,2,0:T(8,128)(2,1)S(1)}, bf16[1,32,1,2,128]{4,1,3,2,0:T(8,128)(2,1)S(1)}, u32[]{:S(2)}, u32[]{:S(2)}) collective-permute-start(bf16[1,32,1,2,128]{4,1,3,2,0:T(8,128)(2,1)S(1)} %get-tuple-element.46), channel_id=1, source_target_pairs={{0,12},{4,8},{8,4},{12,0},{16,28},{20,24},{24,20},{28,16},{1,13},{... | collective-permute-start | bytes 49160 | tf_op jit(solution)/shard_map/ppermute | solution.py:74
  23.7 6.6 %collective-permute-start.17 = (bf16[1,32,1,2,128]{4,1,3,2,0:T(8,128)(2,1)S(1)}, bf16[1,32,1,2,128]{4,1,3,2,0:T(8,128)(2,1)S(1)}, u32[]{:S(2)}, u32[]{:S(2)}) collective-permute-start(bf16[1,32,1,2,128]{4,1,3,2,0:T(8,128)(2,1)S(1)} %get-tuple-element.45), channel_id=1, source_target_pairs={{0,16},{4,20},{8,24},{12,28},{16,0},{20,4},{24,8},{28,12},{1,17},{... | collective-permute-start | bytes 49160 | tf_op jit(solution)/shard_map/ppermute | solution.py:74
  23.8 6.5 %collective-permute-start.18 = (bf16[1,32,1,2,128]{4,1,3,2,0:T(8,128)(2,1)S(1)}, bf16[1,32,1,2,128]{4,1,3,2,0:T(8,128)(2,1)S(1)}, u32[]{:S(2)}, u32[]{:S(2)}) collective-permute-start(bf16[1,32,1,2,128]{4,1,3,2,0:T(8,128)(2,1)S(1)} %get-tuple-element.44), channel_id=1, source_target_pairs={{0,20},{4,16},{8,28},{12,24},{16,4},{20,0},{24,12},{28,8},{1,21},{... | collective-permute-start | bytes 49160 | tf_op jit(solution)/shard_map/ppermute | solution.py:74
  27.0 4.4 %collective-permute-start.19 = (bf16[1,32,1,2,128]{4,1,3,2,0:T(8,128)(2,1)S(1)}, bf16[1,32,1,2,128]{4,1,3,2,0:T(8,128)(2,1)S(1)}, u32[]{:S(2)}, u32[]{:S(2)}) collective-permute-start(bf16[1,32,1,2,128]{4,1,3,2,0:T(8,128)(2,1)S(1)} %get-tuple-element.43), channel_id=1, source_target_pairs={{0,24},{4,28},{8,16},{12,20},{16,8},{20,12},{24,0},{28,4},{1,25},{... | collective-permute-start | bytes 49160 | tf_op jit(solution)/shard_map/ppermute | solution.py:74
  27.1 5.5 %collective-permute-start.20 = (bf16[1,32,1,2,128]{4,1,3,2,0:T(8,128)(2,1)S(1)}, bf16[1,32,1,2,128]{4,1,3,2,0:T(8,128)(2,1)S(1)}, u32[]{:S(2)}, u32[]{:S(2)}) collective-permute-start(bf16[1,32,1,2,128]{4,1,3,2,0:T(8,128)(2,1)S(1)} %get-tuple-element.42), channel_id=1, source_target_pairs={{0,28},{4,24},{8,20},{12,16},{16,12},{20,8},{24,4},{28,0},{1,29},{... | collective-permute-start | bytes 49160 | tf_op jit(solution)/shard_map/ppermute | solution.py:74
  33.2 3.2 %collective-permute-start.1 = (bf16[32,8,2,128]{3,2,1,0:T(2,128)(2,1)S(1)}, bf16[32,8,2,128]{3,2,1,0:T(2,128)(2,1)}, u32[]{:S(2)}, u32[]{:S(2)}) collective-permute-start(bf16[32,8,2,128]{3,2,1,0:T(2,128)(2,1)S(1)} %param.1), channel_id=1, source_target_pairs={{8,0},{12,4},{16,8},{20,12},{24,16},{28,20},{9,1},{13,5},{17,9},{2... | collective-permute-start | bytes 393224 | tf_op jit(solution)/shard_map/cond/branch_1_fun/ppermute | solution.py:33
  36.5 1.3 collective-permute-start.13
  118.8 32.9 %copy-start.1 = (bf16[8,32768]{1,0:T(8,128)(2,1)S(1)}, bf16[8,32768]{1,0:T(8,128)(2,1)}, u32[]{:S(2)}) copy-start(bf16[8,32768]{1,0:T(8,128)(2,1)} %reduce-scatter.4.cloned.1.call-done) | copy-start | bytes 1572868
  120.0 15.4 %collective-permute-start.21 = (bf16[2,8,128,128]{3,2,1,0:T(8,128)(2,1)S(1)}, bf16[2,8,128,128]{3,2,1,0:T(8,128)(2,1)S(1)}, u32[]{:S(2)}, u32[]{:S(2)}) collective-permute-start(bf16[2,8,128,128]{3,2,1,0:T(8,128)(2,1)S(1)} %copy.83), channel_id=1, source_target_pairs={{0,4},{4,8},{8,12},{12,16},{16,20},{20,24},{24,28},{1,5},{5,9},{9,... | collective-permute-start | bytes 1572872 | tf_op jit(solution)/shard_map/ppermute | solution.py:33
  136.6 13.7 %collective-permute-start.22 = (bf16[2,8,128,128]{3,2,1,0:T(8,128)(2,1)S(1)}, bf16[2,8,128,128]{3,2,1,0:T(8,128)(2,1)S(1)}, u32[]{:S(2)}, u32[]{:S(2)}) collective-permute-start(bf16[2,8,128,128]{3,2,1,0:T(8,128)(2,1)S(1)} %broadcast_select_fusion.1), channel_id=1, source_target_pairs={{0,8},{4,12},{8,16},{12,20},{16,24},{20,28},{1,9},{5,13},{9,17},{1... | collective-permute-start | bytes 1572872 | tf_op jit(solution)/shard_map/ppermute | solution.py:33
  150.4 27.9 %collective-permute-start.23 = (bf16[2,8,128,128]{3,2,1,0:T(8,128)(2,1)S(1)}, bf16[2,8,128,128]{3,2,1,0:T(8,128)(2,1)S(1)}, u32[]{:S(2)}, u32[]{:S(2)}) collective-permute-start(bf16[2,8,128,128]{3,2,1,0:T(8,128)(2,1)S(1)} %broadcast_select_fusion.2), channel_id=1, source_target_pairs={{0,16},{4,20},{8,24},{12,28},{1,17},{5,21},{9,25},{13,29},{2,18},{... | collective-permute-start | bytes 1572872 | tf_op jit(solution)/shard_map/ppermute | solution.py:33
Sparse Core Ops, SparseCore 0:
  73.4 45.3 reduce-scatter.3
